TPU v7x, 32 devices: a whole 2x2x4 slice. The times are simulated.
32 devices in a mesh: groups: 2 (over y), row: 4 (over z), col: 2 (over x), rep: 2 (over core).
Axes of the slice: x: 2, y: 2, z: 4, core: 2. Of those that a mesh axis runs over, the one named last changes fastest.
Arguments:
- left_panel: float32 [192512, 2048], P(('groups', 'row', 'col', 'rep')), parts along dimension 0, may hold values from -0.02734375 to 0.02734375
- earlier: float32 [192512, 256], P(('groups', 'row', 'col', 'rep')), parts along dimension 0, may hold values from -6 to 6
- diag_block: float32 [4096, 2048], P(('groups', 'col'), 'row'), parts along dimension 0, as said below
- chosen: int32 [512], P(('groups', 'row', 'rep')), parts along dimension 0, may hold values from 0 to 2047
Outputs:
- marginal: float32 [4096, 256], P(('groups', 'col'), ('row', 'rep')), parts along dimension 0
- updated: float32 [192512, 256], P(('groups', 'row', 'col', 'rep')), parts along dimension 0
There are 2 independent parts, one for each index of `groups`. A program takes and returns all parts, laid end to end along the dimension named above; each array names one. Nothing has to cross between parts.
Inputs may be any that keep to these rules, and one draw needn't show every extreme that they name: diag_block is lower triangular with diagonal entries from 1 to 2.
All inputs are finite; a program needn't handle non-finite values.
Results may differ from a plain program's by a relative error of at most 0.00029.
Values sent between devices are 32-bit elements; how exact they have to be, the bound alone decides.
No kernel may reach another device: no remote copies, remote signals or barrier semaphores. Data moves between devices by JAX's collectives and lax.ppermute only.
A program may use at most 192 MiB of HBM per device.

v0:
```python
import jax
import jax.numpy as jnp
from jax import lax
from jax.sharding import PartitionSpec as P

exact_mode = lax.Precision.HIGHEST


def spread(block, axis, holder):
    block = jnp.where(lax.axis_index(axis) == holder, block, jnp.zeros_like(block))
    return lax.psum(block, axis)


def local(left_panel, earlier, diag_block, chosen):
    row_count = lax.axis_size("row")
    col_count = lax.axis_size("col")
    pair_count = lax.axis_size("rep")
    position = lax.axis_index("col")
    local_rows, slab_size = left_panel.shape
    height = slab_size // col_count
    total_cols = earlier.shape[1]
    narrow = total_cols // (row_count * pair_count)
    panel_tiles = left_panel.reshape(local_rows, col_count, height)
    earlier_tiles = earlier.reshape(local_rows, row_count, pair_count, narrow)
    products = jnp.einsum(
        "pca,prqb->rcqab",
        panel_tiles,
        earlier_tiles,
        precision=exact_mode,
        preferred_element_type=jnp.float32,
    )
    products = products.reshape(row_count * col_count * pair_count, height * narrow)
    summed = lax.psum_scatter(products, ("row", "col", "rep"), scatter_dimension=0, tiled=True)
    coupled = summed.reshape(height, narrow)
    rows_here = position * height + jnp.arange(height, dtype=jnp.int32)
    unit_cols = (rows_here[:, None] == chosen[None, :]).astype(jnp.float32)
    right_side = unit_cols - coupled
    row_block = lax.all_gather(diag_block, "row", axis=1, tiled=True)
    diag_tile = lax.dynamic_slice_in_dim(row_block, position * height, height, 1)
    empty = jnp.zeros((height, narrow), jnp.float32)

    def forward_step(level, carry):
        carried, solved = carry
        candidate = lax.linalg.triangular_solve(
            diag_tile, right_side - carried, left_side=True, lower=True
        )
        panel = spread(candidate, "col", level)
        solved = jnp.where(level == position, panel, solved)
        coupling_tile = lax.dynamic_slice_in_dim(row_block, level * height, height, 1)
        update = jnp.dot(
            coupling_tile, panel, precision=exact_mode, preferred_element_type=jnp.float32
        )
        carried = carried + jnp.where(position > level, update, 0.0)
        return (carried, solved)

    carried_fwd, forward = lax.fori_loop(0, col_count, forward_step, (empty, empty))

    def backward_step(counter, carry):
        carried, result = carry
        level = col_count - 1 - counter
        candidate = lax.linalg.triangular_solve(
            diag_tile, forward - carried, left_side=True, lower=True, transpose_a=True
        )
        result = jnp.where(level == position, candidate, result)
        spread_rows = jnp.dot(
            row_block.T, candidate, precision=exact_mode, preferred_element_type=jnp.float32
        )
        spread_rows = spread(spread_rows, "col", level)
        update = lax.dynamic_slice_in_dim(spread_rows, position * height, height, 0)
        carried = carried + jnp.where(position < level, update, 0.0)
        return (carried, result)

    carried_bwd, marginal = lax.fori_loop(0, col_count, backward_step, (empty, empty))
    gathered = lax.all_gather(
        marginal.reshape(1, height * narrow), ("row", "col", "rep"), axis=0, tiled=True
    )
    gathered = gathered.reshape(row_count, col_count, pair_count, height, narrow)
    correction = jnp.einsum(
        "pca,rcqab->prqb",
        panel_tiles,
        gathered,
        precision=exact_mode,
        preferred_element_type=jnp.float32,
    )
    updated = earlier - correction.reshape(local_rows, total_cols)
    return (marginal, updated)


def solution(mesh):
    placed = (
        P(("groups", "row", "col", "rep"), None),
        P(("groups", "row", "col", "rep"), None),
        P(("groups", "col"), "row"),
        P(("groups", "row", "rep")),
    )
    return jax.shard_map(
        local,
        mesh=mesh,
        in_specs=placed,
        out_specs=(P(("groups", "col"), ("row", "rep")), P(("groups", "row", "col", "rep"), None)),
        check_vma=False,
    )
```

profile of v0, /device:TPU:0, one launch (start us, length us, event | category | flops | bytes accessed | tf_op | source)
XLA Modules:
  0.0 1081.9 jit_solution(3599358955177712432)
XLA Ops:
  8.0 6.5 copy.22
  14.6 62.0 %reshape.191 = f32[6016,2,1024]{2,1,0:T(2,128)} reshape(f32[6016,2048]{1,0:T(8,128)} %param.8) | data formatting | bytes 98566144 | tf_op jit(solution)/shard_map/reshape | solution.py:23
  76.6 66.4 %fusion.106 = f32[4,2,2,1024,32]{3,4,1,2,0:T(8,128)S(1)} fusion(f32[6016,4,2,32,1]{0,3,4,2,1:T(8,128)} %bitcast.282, f32[6016,2,1024,1,1]{2,1,0,4,3:T(2,128)} %bitcast.280), kind=kOutput, calls=%fused_computation.192 | convolution fusion | flops 37849399296 | bytes 57540608 | tf_op jit(solution)/shard_map/pca,prqb->rcqab/dot_general | solution.py:25
  143.0 4.6 copy.24
  147.6 7.0 reshape.192
  155.8 232.2 %all-reduce.5.cloned.1.call-done = f32[16,32768]{1,0:T(8,128)} async-done(((f32[16,32768]{1,0:T(8,128)}), f32[16,32768]{1,0:T(8,128)}) %all-reduce.5.cloned.1.call-update) | async-done | bytes 2097168
  390.9 6.9 fusion.105
  397.8 23.6 %while.41 = (s32[]{:T(128)}, f32[1024,1024]{1,0:T(8,128)}, s32[8,2]{0,1:T(2,128)S(1)}, f32[8,128,128]{2,1,0:T(8,128)S(1)}, s32[]{:T(128)}) while((s32[]{:T(128)}, f32[1024,1024]{1,0:T(8,128)}, s32[8,2]{0,1:T(2,128)S(1)}, f32[8,128,128]{2,1,0:T(8,128)S(1)}, s32[]{:T(128)}) %tuple.158), condition=%wide.while_cond, body=%wide.while_body.sunk | while | flops 2 | bytes 131189 | solution.py:44
  398.5 2.3 bitcast_dynamic-update-slice_fusion.2
  401.4 2.3 bitcast_dynamic-update-slice_fusion.2
  404.4 2.3 bitcast_dynamic-update-slice_fusion.2
  421.4 78.6 %custom-call.21 = f32[8,128,128]{1,2,0:T(8,128)S(1)} custom-call(f32[8,128,128]{2,1,0:T(8,128)S(1)} %get-tuple-element.500), custom_call_target="InvertDiagBlocksLowerTriangular" | custom-call | tf_op jit(solution)/shard_map/while/body/eval_jaxpr/triangular_solve | solution.py:44
  500.2 89.2 %while.42 = (s32[]{:T(128)}, f32[1024,32]{0,1:T(8,128)S(1)}, f32[1024,32]{0,1:T(8,128)S(1)}, s32[]{:T(128)}, f32[1024,2048]{1,0:T(8,128)}, /*index=5*/f32[1024,3...) while((s32[]{:T(128)}, f32[1024,32]{0,1:T(8,128)S(1)}, ...), condition=%wide.region_3.4_spmd.clone, body=%wide.region_1.3_spmd.clone.sunk | while | flops 631648256 | bytes 18481448 | solution.py:56
  500.3 4.8 fusion.223
  516.9 20.9 %all-reduce.7.cloned.1.call-done = f32[1024,32]{0,1:T(8,128)} async-done(((f32[1024,32]{0,1:T(8,128)}), f32[1024,32]{0,1:T(8,128)}) %all-reduce.7.cloned.1.call-update) | async-done | bytes 131088 | tf_op jit(solution)/shard_map/while/body/eval_jaxpr/psum | solution.py:11
  538.8 6.1 fusion.225
  544.9 4.8 fusion.223
  561.6 21.7 %all-reduce.7.cloned.1.call-done = f32[1024,32]{0,1:T(8,128)} async-done(((f32[1024,32]{0,1:T(8,128)}), f32[1024,32]{0,1:T(8,128)}) %all-reduce.7.cloned.1.call-update) | async-done | bytes 131088 | tf_op jit(solution)/shard_map/while/body/eval_jaxpr/psum | solution.py:11
  583.3 6.1 fusion.225
  589.4 96.0 %while.43 = (s32[]{:T(128)}, f32[1024,32]{0,1:T(8,128)S(1)}, f32[1024,32]{0,1:T(8,128)S(1)}, s32[]{:T(128)}, f32[1024,32]{0,1:T(8,128)S(1)}, /*index=5*/f32[1024...) while((s32[]{:T(128)}, f32[1024,32]{0,1:T(8,128)S(1)}, ...), condition=%wide.region_6.7_spmd.clone, body=%wide.region_4.6_spmd.clone.sunk | while | flops 1034366976 | bytes 24002808 | solution.py:73
  589.9 4.8 fusion.255
  604.9 7.9 fusion.258
  612.8 24.3 %all-reduce.9.cloned.1.call-done = f32[2048,32]{0,1:T(8,128)} async-done(((f32[2048,32]{0,1:T(8,128)}), f32[2048,32]{0,1:T(8,128)}) %all-reduce.9.cloned.1.call-update) | async-done | bytes 262160 | tf_op jit(solution)/shard_map/while/body/eval_jaxpr/psum | solution.py:11
  638.1 4.8 fusion.255
  653.1 7.9 fusion.258
  661.1 23.4 %all-reduce.9.cloned.1.call-done = f32[2048,32]{0,1:T(8,128)} async-done(((f32[2048,32]{0,1:T(8,128)}), f32[2048,32]{0,1:T(8,128)}) %all-reduce.9.cloned.1.call-update) | async-done | bytes 262160 | tf_op jit(solution)/shard_map/while/body/eval_jaxpr/psum | solution.py:11
  686.6 43.5 %all-gather.6.cloned.1.call-done = f32[16,1,32768]{2,1,0:T(1,128)} async-done(((f32[1,1,32768]{2,1,0:T(1,128)}), f32[16,1,32768]{2,1,0:T(1,128)}) %all-gather.6.cloned.1.call-update) | async-done | bytes 2097168 | tf_op jit(solution)/shard_map/all_gather | solution.py:74
  730.2 6.6 reduce.1
  736.8 4.7 reshape.195
  741.5 318.1 %fusion.100 = f32[4,2,32,6016,1]{3,2,1,4,0:T(8,128)} fusion(f32[4,2,2,1024,32]{4,3,2,1,0:T(8,128)} %reshape.195, f32[6016,2,1024,1,1]{2,1,0,4,3:T(2,128)} %bitcast.281), kind=kOutput, calls=%fused_computation.185 | convolution fusion | flops 37849399296 | bytes 57540608 | tf_op jit(solution)/shard_map/pca,rcqab->prqb/dot_general | solution.py:78
  1059.7 6.5 copy.31
  1066.2 8.0 sub.41
  (174 shorter events, 68.4 us)
Async XLA Ops:
  8.0 380.1 %all-reduce.5.cloned.1.call-start = ((), (), s32[]{:S(2)}) async-start(), calls=%async_computation.2 | async-start | bytes 4194304
  154.5 0.7 copy-start.2
  154.5 235.9 %copy-start.1 = (s32[32]{0:T(128)S(1)}, s32[32]{0:T(128)}, u32[]{:S(2)}) copy-start(s32[32]{0:T(128)} %param.11) | copy-start | bytes 388
  154.6 236.3 %all-gather.4.cloned.1.call-start = ((), (), s32[]{:S(2)}) async-start(), calls=%async_computation | async-start | bytes 10485760 | tf_op jit(solution)/shard_map/all_gather | solution.py:38
  500.2 37.6 %all-reduce.7.cloned.1.call-start = ((), (), s32[]{:S(2)}) async-start(), calls=%async_computation.3 | async-start | bytes 262144 | tf_op jit(solution)/shard_map/while/body/eval_jaxpr/psum | solution.py:11
  544.9 38.3 %all-reduce.7.cloned.1.call-start = ((), (), s32[]{:S(2)}) async-start(), calls=%async_computation.3 | async-start | bytes 262144 | tf_op jit(solution)/shard_map/while/body/eval_jaxpr/psum | solution.py:11
  589.8 47.3 %all-reduce.9.cloned.1.call-start = ((), (), s32[]{:S(2)}) async-start(), calls=%async_computation.4 | async-start | bytes 524288 | tf_op jit(solution)/shard_map/while/body/eval_jaxpr/psum | solution.py:11
  638.1 46.4 %all-reduce.9.cloned.1.call-start = ((), (), s32[]{:S(2)}) async-start(), calls=%async_computation.4 | async-start | bytes 524288 | tf_op jit(solution)/shard_map/while/body/eval_jaxpr/psum | solution.py:11
  685.4 56.1 %copy-start = (f32[1024,32]{0,1:T(8,128)}, f32[1024,32]{0,1:T(8,128)S(1)}, u32[]{:S(2)}) copy-start(f32[1024,32]{0,1:T(8,128)S(1)} %get-tuple-element.489) | copy-start | bytes 393220
  685.4 44.7 %all-gather.6.cloned.1.call-start = ((), (), s32[]{:S(2)}) async-start(), calls=%async_computation.1 | async-start | bytes 2228224 | tf_op jit(solution)/shard_map/all_gather | solution.py:74
Sparse Core Ops, SparseCore 0:
  154.7 233.3 all-reduce.4
  517.0 20.7 all-reduce.6
  561.7 21.5 all-reduce.6
  612.9 24.1 all-reduce.8
  661.1 23.2 all-reduce.8
  688.7 41.4 all-gather.5
Sparse Core Ops, SparseCore 1:
  156.6 157.0 all-gather.3
where the time goes:
time: 1090 us; the launch traced here: 1080 us
  matrix products  454 us (42%)
  waiting for transfers between devices  367 us (34%)
  other arithmetic  124 us (11%)
  local copies, waits for them, and re-layouts  120 us (11%)
  between operations  15.9 us (1%)
    dot_general x1, matrix products, local(): jnp.einsum('pca,rcqab->prqb', panel_tiles, gathered, precision=exact_mode...  318 us
    unnamed x4, waiting for transfers between devices  233 us
    another operation x5, other arithmetic, forward_step(): lax.linalg.triangular_solve(diag_tile, right_side - carried, left_side=Tr...  95.1 us
    psum x4, waiting for transfers between devices, spread(): return lax.psum(block, axis)  90.3 us
    dot_general x1, matrix products, local(): jnp.einsum('pca,prqb->rcqab', panel_tiles, earlier_tiles, precision=exact...  66.4 us
    reshape x1, local copies, waits for them, and re-layouts, local(): panel_tiles = left_panel.reshape(local_rows, col_count, height)  62 us
    all_gather x1, waiting for transfers between devices, local(): lax.all_gather(marginal.reshape(1, height * narrow), ('row', 'col', 'rep'...  43.5 us
    another operation x24, local copies, waits for them, and re-layouts  23.4 us
  transfers between devices with their start and end apart: 7, of which 6 were waited for; matrix products, arithmetic and copies ran while one was open for 0% of the time, Pallas kernels for 0%

commit v1 on v0

--- a/solution.py
+++ b/solution.py
@@ -6,9 +6,15 @@
 exact_mode = lax.Precision.HIGHEST
 
 
+def gather_and_add(x, name):
+    parts = lax.all_gather(x, name, axis=0, tiled=False)
+    total = parts.sum(axis=0)
+    return total
+
+
 def spread(block, axis, holder):
     block = jnp.where(lax.axis_index(axis) == holder, block, jnp.zeros_like(block))
-    return lax.psum(block, axis)
+    return gather_and_add(block, axis)
 
 
 def local(left_panel, earlier, diag_block, chosen):

time: 1090 us -> 1000 us (0.917)
  waiting for transfers between devices: 367 us -> 273 us
  blocking collectives: 0 us -> 25.4 us
  matrix products: 454 us -> 439 us
    psum x4 -> x0, waiting for transfers between devices: 90.3 us -> none  [spread(): return lax.psum(block, axis)]
    all_gather x0 -> x4, blocking collectives: none -> 25.4 us  [gather_and_add(): parts = lax.all_gather(x, name, axis=0, tiled=False)]
    another operation x30, matrix products: 22 us -> 8.47 us  [forward_step(): lax.linalg.triangular_solve(diag_tile, right_side - carried, left_side=Tr...]
  transfers between devices with their start and end apart: 7 -> 3, of which waited for: 6 -> 2; matrix products, arithmetic and copies ran while one was open for 0% -> 0% of each run, Pallas kernels for 0% -> 0%
where the time goes in v1:
time: 1000 us; the launch traced here: 992 us
  matrix products  439 us (44%)
  waiting for transfers between devices  273 us (27%)
  local copies, waits for them, and re-layouts  119 us (12%)
  other arithmetic  117 us (12%)
  blocking collectives  25.4 us (3%)
  between operations  15.8 us (2%)
    dot_general x1, matrix products, local(): jnp.einsum('pca,rcqab->prqb', panel_tiles, gathered, precision=exact_mode...  318 us
    unnamed x4, waiting for transfers between devices  233 us
    another operation x5, other arithmetic, forward_step(): lax.linalg.triangular_solve(diag_tile, right_side - carried, left_side=Tr...  90.8 us
    dot_general x1, matrix products, local(): jnp.einsum('pca,prqb->rcqab', panel_tiles, earlier_tiles, precision=exact...  66.4 us
    reshape x1, local copies, waits for them, and re-layouts, local(): panel_tiles = left_panel.reshape(local_rows, col_count, height)  62 us
    all_gather x1, waiting for transfers between devices, local(): lax.all_gather(marginal.reshape(1, height * narrow), ('row', 'col', 'rep'...  40.9 us
    all_gather x4, blocking collectives, gather_and_add(): parts = lax.all_gather(x, name, axis=0, tiled=False)  25.4 us
    another operation x24, local copies, waits for them, and re-layouts  22.2 us
  transfers between devices with their start and end apart: 3, of which 2 were waited for; matrix products, arithmetic and copies ran while one was open for 0% of the time, Pallas kernels for 0%

profile of v1, /device:TPU:0, one launch (start us, length us, event | category | flops | bytes accessed | tf_op | source)
XLA Modules:
  0.0 992.1 jit_solution(8300861370746132185)
XLA Ops:
  8.0 6.5 copy.22
  14.6 62.0 %reshape.338 = f32[6016,2,1024]{2,1,0:T(2,128)} reshape(f32[6016,2048]{1,0:T(8,128)} %param.8) | data formatting | bytes 98566144 | tf_op jit(solution)/shard_map/reshape | solution.py:29
  76.6 66.4 %fusion.112 = f32[4,2,2,1024,32]{3,4,1,2,0:T(8,128)S(1)} fusion(f32[6016,4,2,32,1]{0,3,4,2,1:T(8,128)} %bitcast.347, f32[6016,2,1024,1,1]{2,1,0,4,3:T(2,128)} %bitcast.345), kind=kOutput, calls=%fused_computation.192 | convolution fusion | flops 37849399296 | bytes 57540608 | tf_op jit(solution)/shard_map/pca,prqb->rcqab/dot_general | solution.py:31
  143.0 4.6 copy.24
  147.6 7.0 reshape.339
  156.1 232.0 %all-reduce.3.cloned.1.call-done = f32[16,32768]{1,0:T(8,128)} async-done(((f32[16,32768]{1,0:T(8,128)}), f32[16,32768]{1,0:T(8,128)}) %all-reduce.3.cloned.1.call-update) | async-done | bytes 2097168
  390.8 6.9 fusion.111
  397.8 22.4 %while.41 = (s32[]{:T(128)}, f32[1024,1024]{1,0:T(8,128)}, s32[8,2]{0,1:T(2,128)S(1)}, f32[8,128,128]{2,1,0:T(8,128)S(1)}, s32[]{:T(128)}) while((s32[]{:T(128)}, f32[1024,1024]{1,0:T(8,128)}, s32[8,2]{0,1:T(2,128)S(1)}, f32[8,128,128]{2,1,0:T(8,128)S(1)}, s32[]{:T(128)}) %tuple.166), condition=%wide.while_cond, body=%wide.while_body.sunk | while | flops 2 | bytes 131189 | solution.py:50
  398.4 2.2 bitcast_dynamic-update-slice_fusion.2
  401.2 2.2 bitcast_dynamic-update-slice_fusion.2
  404.0 2.2 bitcast_dynamic-update-slice_fusion.2
  420.1 78.6 %custom-call.21 = f32[8,128,128]{1,2,0:T(8,128)S(1)} custom-call(f32[8,128,128]{2,1,0:T(8,128)S(1)} %get-tuple-element.500), custom_call_target="InvertDiagBlocksLowerTriangular" | custom-call | tf_op jit(solution)/shard_map/while/body/eval_jaxpr/triangular_solve | solution.py:50
  498.9 38.2 %while.42 = (s32[]{:T(128)}, f32[1024,32]{0,1:T(8,128)S(1)}, f32[1024,32]{0,1:T(8,128)S(1)}, s32[]{:T(128)}, f32[1024,2048]{1,0:T(8,128)}, /*index=5*/f32[1024,3...) while((s32[]{:T(128)}, f32[1024,32]{0,1:T(8,128)S(1)}, ...), condition=%wide.region_3.4_spmd.clone, body=%wide.region_1.3_spmd.clone.sunk | while | flops 631648256 | bytes 18645260 | solution.py:62
  499.2 2.7 fusion.229
  506.2 5.6 all_gather.47
  511.9 6.1 fusion.231
  518.3 2.7 fusion.229
  525.3 5.6 all_gather.47
  531.0 6.1 fusion.231
  537.1 61.2 %while.43 = (s32[]{:T(128)}, f32[1024,32]{0,1:T(8,128)S(1)}, f32[1024,32]{0,1:T(8,128)S(1)}, s32[]{:T(128)}, f32[1024,32]{0,1:T(8,128)S(1)}, /*index=5*/f32[1024...) while((s32[]{:T(128)}, f32[1024,32]{0,1:T(8,128)S(1)}, ...), condition=%wide.region_6.7_spmd.clone, body=%wide.region_4.6_spmd.clone.sunk | while | flops 1034366976 | bytes 25051364 | solution.py:79
  537.5 4.8 fusion.261
  552.5 7.2 fusion.264
  559.7 7.0 all-gather.4
  567.9 4.8 fusion.261
  582.9 7.2 fusion.264
  590.1 7.0 all-gather.4
  599.5 40.9 %all-gather.10.cloned.1.call-done = f32[16,1,32768]{2,1,0:T(1,128)} async-done(((f32[1,1,32768]{2,1,0:T(1,128)}), f32[16,1,32768]{2,1,0:T(1,128)}) %all-gather.10.cloned.1.call-update) | async-done | bytes 2097168 | tf_op jit(solution)/shard_map/all_gather | solution.py:80
  640.4 6.6 reduce.1
  647.0 4.7 reshape.342
  651.8 318.1 %fusion.106 = f32[4,2,32,6016,1]{3,2,1,4,0:T(8,128)} fusion(f32[4,2,2,1024,32]{4,3,2,1,0:T(8,128)} %reshape.342, f32[6016,2,1024,1,1]{2,1,0,4,3:T(2,128)} %bitcast.346), kind=kOutput, calls=%fused_computation.185 | convolution fusion | flops 37849399296 | bytes 57540608 | tf_op jit(solution)/shard_map/pca,rcqab->prqb/dot_general | solution.py:84
  969.9 6.5 copy.31
  976.5 8.0 sub.41
  (186 shorter events, 52.1 us)
Async XLA Ops:
  8.0 380.1 %all-reduce.3.cloned.1.call-start = ((), (), s32[]{:S(2)}) async-start(), calls=%async_computation.2 | async-start | bytes 4194304
  154.5 0.9 copy-start.2
  154.5 235.9 %copy-start.1 = (s32[32]{0:T(128)S(1)}, s32[32]{0:T(128)}, u32[]{:S(2)}) copy-start(s32[32]{0:T(128)} %param.11) | copy-start | bytes 388
  154.6 236.2 %all-gather.8.cloned.1.call-start = ((), (), s32[]{:S(2)}) async-start(), calls=%async_computation | async-start | bytes 10485760 | tf_op jit(solution)/shard_map/all_gather | solution.py:44
  155.2 485.2 %all-gather.10.cloned.1.call-start = ((), (), s32[]{:S(2)}) async-start(), calls=%async_computation.1 | async-start | bytes 2228224 | tf_op jit(solution)/shard_map/all_gather | solution.py:80
  598.4 53.4 %copy-start = (f32[1024,32]{0,1:T(8,128)}, f32[1024,32]{0,1:T(8,128)S(1)}, u32[]{:S(2)}) copy-start(f32[1024,32]{0,1:T(8,128)S(1)} %get-tuple-element.489) | copy-start | bytes 393220
Sparse Core Ops, SparseCore 0:
  154.7 233.3 all-reduce.2
  599.6 40.7 all-gather.9
Sparse Core Ops, SparseCore 1:
  156.6 157.0 all-gather.7
